TPU v7x, 256 devices: a whole 4x4x8 slice. The times are simulated.
256 devices in a mesh: sec: 32 (over z, y), blk: 8 (over x, core).
Axes of the slice: x: 4, y: 4, z: 8, core: 2. Of those that a mesh axis runs over, the one named last changes fastest.
Arguments:
- state_now: float32 [128, 65536], P(None, ('sec', 'blk')), may hold values from -5 to 5
- source: float32 [128, 65536], P(None, ('sec', 'blk')), may hold values from -6 to 6
- fan_gain: float32 [65536], P(('sec', 'blk')), may hold values from 0.5 to 12
- section_block: bfloat16 [65536, 2048], P(('sec', 'blk')), may hold values from -1 to 7
- block_inverse: bfloat16 [65536, 2048], P(('sec', 'blk')), may hold values from -1 to 1
- back_panel: bfloat16 [65536, 128], P(('sec', 'blk')), may hold values from -6 to 6
- ahead_panel: bfloat16 [65536, 128], P(('sec', 'blk')), may hold values from -0.0625 to 0.0625
- interface: int32 [32, 128], P('sec'), may hold values from 0 to 2047, as said below
Outputs:
- new_state: float32 [128, 65536], P(None, ('sec', 'blk'))
Inputs may be any that keep to these rules, and one draw needn't show every extreme that they name: `interface`: entries of one section are distinct; entry p lies in [p * 16, (p + 1) * 16).
All inputs are finite; a program needn't handle non-finite values.
Results may differ from a plain program's by a relative error of at most 0.0063.
Values may be sent and summed in bfloat16 or wider, within the bound.
A program may use at most 64 MiB of HBM per device.

v0:
```python
import jax
import jax.numpy as jnp
from jax import lax
from jax.sharding import PartitionSpec as P

KRYLOV = 3
epsilon = 1e-06


def extended(x, sides, width):
    for axis, dim in sides:
        size, length = (lax.axis_size(axis), x.shape[dim])
        up = [(i, (i + 1) % size) for i in range(size - 1)]
        down = [(j, i) for i, j in up]
        last = lax.slice_in_dim(x, length - width, length, axis=dim)
        first = lax.slice_in_dim(x, 0, width, axis=dim)
        before = lax.ppermute(last, axis, up)
        after = lax.ppermute(first, axis, down)
        x = jnp.concatenate([before, x, after], axis=dim)
    return x


def entering(value, axis, join, neutral):
    count, mine = (lax.axis_size(axis), lax.axis_index(axis))
    pieces = jax.tree.map(lambda part: lax.all_gather(part, axis), value)
    so_far = jax.tree.map(
        lambda part, zero: jnp.full_like(part, 0) + jnp.asarray(zero, part.dtype), value, neutral
    )

    def step(position, so_far):
        longer = join(so_far, jax.tree.map(lambda part: part[position], pieces))
        return jax.tree.map(lambda new, old: jnp.where(position < mine, new, old), longer, so_far)

    return lax.fori_loop(0, count - 1, step, so_far)


def least_squares(hessen, beta):
    cases = hessen.shape[0]
    depth = hessen.shape[2]
    rhs = jnp.zeros((cases, depth + 1), jnp.float32).at[:, 0].set(beta)
    upper = hessen
    for column in range(depth):
        upper_row = upper[:, column, :]
        lower_row = upper[:, column + 1, :]
        radius = jnp.sqrt(upper_row[:, column] ** 2 + lower_row[:, column] ** 2)
        cosine = upper_row[:, column] / radius
        sine_term = lower_row[:, column] / radius
        upper = upper.at[:, column, :].set(
            cosine[:, None] * upper_row + sine_term[:, None] * lower_row
        )
        upper = upper.at[:, column + 1, :].set(
            -sine_term[:, None] * upper_row + cosine[:, None] * lower_row
        )
        first_rhs = rhs[:, column]
        second_rhs = rhs[:, column + 1]
        rhs = rhs.at[:, column].set(cosine * first_rhs + sine_term * second_rhs)
        rhs = rhs.at[:, column + 1].set(-sine_term * first_rhs + cosine * second_rhs)
    weights = jnp.zeros((cases, depth), jnp.float32)
    for column in reversed(range(depth)):
        remain = rhs[:, column] - jnp.sum(
            upper[:, column, column + 1 :] * weights[:, column + 1 :], axis=1
        )
        weights = weights.at[:, column].set(remain / upper[:, column, column])
    return weights


def local(
    state_now, source, fan_gain, section_block, block_inverse, back_panel, ahead_panel, interface
):
    highest = lax.Precision.HIGHEST
    cases, node_rows = state_now.shape
    panel_width = back_panel.shape[1]
    indices = interface[0]
    first_row = lax.axis_index("blk") * node_rows
    selector = (indices[None, :] == first_row + jnp.arange(node_rows)[:, None]).astype(jnp.float32)
    contract = (((1,), (1,)), ((), ()))
    gain_panel = jnp.dot(
        block_inverse,
        lax.all_gather(back_panel, "blk", axis=0, tiled=True),
        preferred_element_type=jnp.float32,
    )
    panel_maps = -lax.psum(jnp.dot(selector.T, gain_panel, precision=highest), "blk")

    def section_terms(dense_part, behind_vals, piece):
        width = piece.shape[1]
        dense_part = lax.dot_general(
            piece, section_block, contract, preferred_element_type=jnp.float32
        )
        picker = (indices[None, :] == jnp.arange(width)[:, None]).astype(jnp.bfloat16)
        behind_vals = jnp.dot(piece, picker, preferred_element_type=jnp.float32)
        return (dense_part, behind_vals)

    def fold_section(carry, piece):
        return section_terms(carry[0], carry[1], piece)

    def operator(vector):
        rounded = vector.astype(jnp.bfloat16)
        empty_dense = jnp.zeros((cases, node_rows), jnp.float32)
        empty_panel = jnp.zeros((cases, panel_width), jnp.float32)
        start_carry = (empty_dense, empty_panel)
        folded = fold_section(start_carry, lax.all_gather(rounded, "blk", axis=1, tiled=True))
        dense_part, behind_vals = folded
        upward = lax.psum(jnp.dot(rounded, ahead_panel, preferred_element_type=jnp.float32), "blk")
        framed = extended(jnp.stack([behind_vals, upward])[None], (("sec", 0),), 1)
        behind = framed[0, 0].astype(jnp.bfloat16)
        ahead_term = framed[2, 1]
        lower_term = lax.dot_general(
            behind, back_panel, contract, preferred_element_type=jnp.float32
        )
        upper_term = jnp.dot(ahead_term, selector.T, precision=highest)
        return dense_part + lower_term + upper_term

    def compose(earlier, later):
        first_map, first_value = earlier
        second_map, second_value = later
        joined_map = jnp.dot(second_map, first_map, precision=highest)
        joined_value = jnp.dot(first_value, second_map.T, precision=highest) + second_value
        return (joined_map, joined_value)

    def lengths(vector):
        return jnp.sqrt(lax.psum(jnp.sum(vector * vector, axis=1), ("sec", "blk")) + epsilon)

    bent = jnp.tanh(state_now)
    residual = source - operator(state_now) - fan_gain[None, :] * bent
    jac_diag = fan_gain[None, :] * (1.0 - bent * bent)
    beta = lengths(residual)
    basis = [residual / beta[:, None]]
    directions = []
    hessen = jnp.zeros((cases, KRYLOV + 1, KRYLOV), jnp.float32)
    for column in range(KRYLOV):
        precondition_rounded = basis[column].astype(jnp.bfloat16)
        precondition_folded = lax.dot_general(
            lax.all_gather(precondition_rounded, "blk", axis=1, tiled=True),
            block_inverse,
            contract,
            preferred_element_type=jnp.float32,
        )
        values = lax.psum(jnp.dot(precondition_folded, selector, precision=highest), "blk")
        identity = (
            jnp.eye(panel_width, dtype=jnp.float32),
            jnp.zeros((cases, panel_width), jnp.float32),
        )
        _, before = entering((panel_maps, values), "sec", compose, identity)
        direction = precondition_folded - lax.dot_general(
            before, gain_panel, contract, precision=highest
        )
        product = operator(direction) + jac_diag * direction
        stacked = jnp.stack(basis)
        projections = lax.psum(jnp.sum(product[None] * stacked, axis=2), ("sec", "blk"))
        product = product - jnp.sum(projections[:, :, None] * stacked, axis=0)
        length = lengths(product)
        hessen = hessen.at[:, : column + 1, column].set(projections.T)
        hessen = hessen.at[:, column + 1, column].set(length)
        basis.append(product / length[:, None])
        directions.append(direction)
    weights = least_squares(hessen, beta)
    update = jnp.zeros_like(state_now)
    for column in range(KRYLOV):
        update = update + weights[:, column : column + 1] * directions[column]
    return state_now + update


def solution(mesh):
    in_specs = (
        P(None, ("sec", "blk")),
        P(None, ("sec", "blk")),
        P(("sec", "blk")),
        P(("sec", "blk"), None),
        P(("sec", "blk"), None),
        P(("sec", "blk"), None),
        P(("sec", "blk"), None),
        P("sec", None),
    )
    out_specs = P(None, ("sec", "blk"))
    return jax.shard_map(local, mesh=mesh, in_specs=in_specs, out_specs=out_specs, check_vma=False)
```

profile of v0, /device:TPU:1, one launch (start us, length us, event | category | flops | bytes accessed | tf_op | source)
XLA Modules:
  0.0 1640.1 jit_solution(12427240941463223437)
XLA Ops:
  9.4 16.2 all_gather.52
  27.1 13.1 all_gather.54
  40.7 34.6 %all-reduce.11.cloned.1.call-done = f32[1,128,128]{1,2,0:T(8,128)} async-done(((f32[1,128,128]{1,2,0:T(8,128)}), f32[1,128,128]{1,2,0:T(8,128)}) %all-reduce.11.cloned.1.call-update) | async-done | bytes 65552 | tf_op jit(solution)/shard_map/psum | solution.py:103
  86.3 83.2 %psum.106 = f32[128]{0:T(128)S(1)} all-reduce(f32[128]{0:T(128)S(1)} %get-tuple-element.720), channel_id=1, replica_groups=mesh['sec'=32,'blk'=8] {'sec','blk'}, use_global_device_ids=true, to_apply=%region_4.0 | all-reduce | flops 128 | bytes 1024 | tf_op jit(solution)/shard_map/psum | solution.py:121
  169.7 13.9 all_gather.53
  185.0 57.8 %all-reduce.23.cloned.1.call-done = (f32[128,128]{1,0:T(8,128)}, f32[1,128,128]{2,1,0:T(8,128)}) async-done(((f32[128,128]{1,0:T(8,128)}, f32[1,128,128]{2,1,0:T(8,128)}), (f32[128,128]{1,0:T(8,128)}, f32[1,128,128]{2,1,0:T(8,128)})) %all-reduce.23.cloned.1.call-update) | async-done | bytes 131088 | tf_op jit(solution)/shard_map/psum | solution.py:82
  244.9 75.7 %all-gather.12.cloned.1.call-done = f32[4096,128]{1,0:T(8,128)} async-done(((f32[128,128]{1,0:T(8,128)}), f32[4096,128]{1,0:T(8,128)}) %all-gather.12.cloned.1.call-update) | async-done | bytes 2097168 | tf_op jit(solution)/shard_map/all_gather | solution.py:25
  320.6 77.6 %all-gather.6.cloned.1.call-done = f32[32,128,128]{2,1,0:T(8,128)} async-done(((f32[1,128,128]{2,1,0:T(8,128)}), f32[32,128,128]{2,1,0:T(8,128)}) %all-gather.6.cloned.1.call-update) | async-done | bytes 2097168 | tf_op jit(solution)/shard_map/all_gather | solution.py:25
  398.3 63.2 %while.64 = (s32[]{:T(128)}, f32[128,128]{0,1:T(8,128)S(1)}, s32[]{:T(128)}, f32[32,128,128]{2,1,0:T(8,128)}, f32[32,128,128]{2,1,0:T(8,128)}, /*index=5*/s32[]{:T(128)}, s32[]{:T(128)}) while((s32[]{:T(128)}, f32[128,128]{0,1:T(8,128)S(1)}, s32[]{:T(128)}, f32[32,128,128]{2,1,0:T(8,128)}, f32[32,128,128]{2,1,0:T(8,128)}, ...), condition=%wide.region_8.9_spmd.clone, body=%wide.region_7.8_spmd.clone.sunk | while | flops 25231364 | bytes 723043 | solution.py:34
  461.8 17.8 %all_gather.59 = bf16[128,2048]{1,0:T(8,128)(2,1)S(1)} all-gather(bf16[128,256]{1,0:T(8,128)(2,1)S(1)} %get-tuple-element.722), channel_id=1, replica_groups=mesh['sec'=32,'blk'=8] {'blk'}, dimensions={1}, use_global_device_ids=true | all-gather | bytes 589824 | tf_op jit(solution)/shard_map/all_gather | solution.py:101
  480.8 57.6 %all-reduce.13.cloned.1.call-done = f32[1,128,128]{2,1,0:T(8,128)} async-done(((f32[1,128,128]{2,1,0:T(8,128)}), f32[1,128,128]{2,1,0:T(8,128)}) %all-reduce.13.cloned.1.call-update) | async-done | bytes 65552 | tf_op jit(solution)/shard_map/psum | solution.py:103
  544.4 4.2 collective-permute-done.3
  549.1 83.2 %psum.110 = f32[1,128]{1,0:T(1,128)S(1)} all-reduce(f32[1,128]{1,0:T(1,128)S(1)} %bitcast.287), channel_id=1, replica_groups=mesh['sec'=32,'blk'=8] {'sec','blk'}, use_global_device_ids=true, to_apply=%region_11.12 | all-reduce | flops 128 | bytes 1024 | tf_op jit(solution)/shard_map/psum | solution.py:149
  632.5 72.3 %psum.111 = f32[128]{0:T(128)S(1)} all-reduce(f32[128]{0:T(128)S(1)} %get-tuple-element.687), channel_id=1, replica_groups=mesh['sec'=32,'blk'=8] {'sec','blk'}, use_global_device_ids=true, to_apply=%region_13.14 | all-reduce | flops 128 | bytes 1024 | tf_op jit(solution)/shard_map/psum | solution.py:121
  705.0 13.6 all_gather.60
  720.1 58.5 %all-reduce.15.cloned.1.call-done = f32[1,128,128]{2,1,0:T(8,128)} async-done(((f32[1,128,128]{2,1,0:T(8,128)}), f32[1,128,128]{2,1,0:T(8,128)}) %all-reduce.15.cloned.1.call-update) | async-done | bytes 65552 | tf_op jit(solution)/shard_map/psum | solution.py:138
  778.7 77.7 %all-gather.8.cloned.1.call-done = f32[32,128,128]{2,1,0:T(8,128)} async-done(((f32[1,128,128]{2,1,0:T(8,128)}), f32[32,128,128]{2,1,0:T(8,128)}) %all-gather.8.cloned.1.call-update) | async-done | bytes 2097168 | tf_op jit(solution)/shard_map/all_gather | solution.py:25
  856.4 63.2 %while.65 = (s32[]{:T(128)}, f32[128,128]{0,1:T(8,128)S(1)}, s32[]{:T(128)}, f32[32,128,128]{2,1,0:T(8,128)}, f32[32,128,128]{2,1,0:T(8,128)}, /*index=5*/s32[]{:T(128)}, s32[]{:T(128)}) while((s32[]{:T(128)}, f32[128,128]{0,1:T(8,128)S(1)}, s32[]{:T(128)}, f32[32,128,128]{2,1,0:T(8,128)}, f32[32,128,128]{2,1,0:T(8,128)}, ...), condition=%wide.region_16.17_spmd.clone, body=%wide.region_15.16_spmd.clone.sunk | while | flops 25231364 | bytes 723043 | solution.py:34
  920.6 17.8 %all_gather.63 = bf16[128,2048]{1,0:T(8,128)(2,1)S(1)} all-gather(bf16[128,256]{1,0:T(8,128)(2,1)S(1)} %get-tuple-element.724), channel_id=1, replica_groups=mesh['sec'=32,'blk'=8] {'blk'}, dimensions={1}, use_global_device_ids=true | all-gather | bytes 589824 | tf_op jit(solution)/shard_map/all_gather | solution.py:101
  939.7 57.4 %all-reduce.17.cloned.1.call-done = f32[1,128,128]{2,1,0:T(8,128)} async-done(((f32[1,128,128]{2,1,0:T(8,128)}), f32[1,128,128]{2,1,0:T(8,128)}) %all-reduce.17.cloned.1.call-update) | async-done | bytes 65552 | tf_op jit(solution)/shard_map/psum | solution.py:103
  1003.1 4.2 collective-permute-done.5
  1007.8 83.2 %psum.114 = f32[2,128]{1,0:T(2,128)S(1)} all-reduce(f32[2,128]{1,0:T(2,128)S(1)} %multiply_reduce_fusion.3), channel_id=1, replica_groups=mesh['sec'=32,'blk'=8] {'sec','blk'}, use_global_device_ids=true, to_apply=%region_19.20 | all-reduce | flops 256 | bytes 2048 | tf_op jit(solution)/shard_map/psum | solution.py:149
  1091.2 72.3 %psum.115 = f32[128]{0:T(128)S(1)} all-reduce(f32[128]{0:T(128)S(1)} %get-tuple-element.683), channel_id=1, replica_groups=mesh['sec'=32,'blk'=8] {'sec','blk'}, use_global_device_ids=true, to_apply=%region_22.23 | all-reduce | flops 128 | bytes 1024 | tf_op jit(solution)/shard_map/psum | solution.py:121
  1163.7 13.6 all_gather.64
  1178.8 58.5 %all-reduce.19.cloned.1.call-done = f32[1,128,128]{2,1,0:T(8,128)} async-done(((f32[1,128,128]{2,1,0:T(8,128)}), f32[1,128,128]{2,1,0:T(8,128)}) %all-reduce.19.cloned.1.call-update) | async-done | bytes 65552 | tf_op jit(solution)/shard_map/psum | solution.py:138
  1243.8 71.1 %all-gather.10.cloned.1.call-done = f32[32,128,128]{2,1,0:T(8,128)} async-done(((f32[1,128,128]{2,1,0:T(8,128)}), f32[32,128,128]{2,1,0:T(8,128)}) %all-gather.10.cloned.1.call-update) | async-done | bytes 2097168 | tf_op jit(solution)/shard_map/all_gather | solution.py:25
  1314.9 63.2 %while.66 = (s32[]{:T(128)}, f32[128,128]{0,1:T(8,128)S(1)}, s32[]{:T(128)}, f32[32,128,128]{2,1,0:T(8,128)}, f32[32,128,128]{2,1,0:T(8,128)}, /*index=5*/s32[]{:T(128)}, s32[]{:T(128)}) while((s32[]{:T(128)}, f32[128,128]{0,1:T(8,128)S(1)}, s32[]{:T(128)}, f32[32,128,128]{2,1,0:T(8,128)}, f32[32,128,128]{2,1,0:T(8,128)}, ...), condition=%wide.region_26.27_spmd.clone, body=%wide.region_25.26_spmd.clone.sunk | while | flops 25231364 | bytes 723043 | solution.py:34
  1379.1 17.8 %all_gather.67 = bf16[128,2048]{1,0:T(8,128)(2,1)S(1)} all-gather(bf16[128,256]{1,0:T(8,128)(2,1)S(1)} %get-tuple-element.726), channel_id=1, replica_groups=mesh['sec'=32,'blk'=8] {'blk'}, dimensions={1}, use_global_device_ids=true | all-gather | bytes 589824 | tf_op jit(solution)/shard_map/all_gather | solution.py:101
  1398.0 57.6 %all-reduce.21.cloned.1.call-done = f32[1,128,128]{2,1,0:T(8,128)} async-done(((f32[1,128,128]{2,1,0:T(8,128)}), f32[1,128,128]{2,1,0:T(8,128)}) %all-reduce.21.cloned.1.call-update) | async-done | bytes 65552 | tf_op jit(solution)/shard_map/psum | solution.py:103
  1461.8 4.2 collective-permute-done.7
  1467.2 83.2 %psum.118 = f32[3,128]{1,0:T(4,128)S(1)} all-reduce(f32[3,128]{1,0:T(4,128)S(1)} %multiply_reduce_fusion.1), channel_id=1, replica_groups=mesh['sec'=32,'blk'=8] {'sec','blk'}, use_global_device_ids=true, to_apply=%region_29.30 | all-reduce | flops 384 | bytes 3072 | tf_op jit(solution)/shard_map/psum | solution.py:149
  1550.6 72.3 %psum.119 = f32[128]{0:T(128)S(1)} all-reduce(f32[128]{0:T(128)S(1)} %multiply_reduce_fusion.4), channel_id=1, replica_groups=mesh['sec'=32,'blk'=8] {'sec','blk'}, use_global_device_ids=true, to_apply=%region_32.33 | all-reduce | flops 128 | bytes 1024 | tf_op jit(solution)/shard_map/psum | solution.py:121
  (521 shorter events, 251.6 us)
Async XLA Ops:
  6.5 33.7 %copy-start = (bf16[256,2048]{1,0:T(8,128)(2,1)S(1)}, bf16[256,2048]{1,0:T(8,128)(2,1)}, u32[]{:S(2)}) copy-start(bf16[256,2048]{1,0:T(8,128)(2,1)} %param.62) | copy-start | bytes 3145732
  6.5 20.0 %copy-start.1 = (bf16[256,2048]{1,0:T(8,128)(2,1)S(1)}, bf16[256,2048]{1,0:T(8,128)(2,1)}, u32[]{:S(2)}) copy-start(bf16[256,2048]{1,0:T(8,128)(2,1)} %param.61) | copy-start | bytes 3145732
  6.5 20.6 %copy-start.3 = (bf16[256,128]{1,0:T(8,128)(2,1)S(1)}, bf16[256,128]{1,0:T(8,128)(2,1)}, u32[]{:S(2)}) copy-start(bf16[256,128]{1,0:T(8,128)(2,1)} %param.63) | copy-start | bytes 196612
  6.5 68.7 %all-reduce.11.cloned.1.call-start = ((), (), s32[]{:S(2)}) async-start(), calls=%async_computation | async-start | bytes 131072 | tf_op jit(solution)/shard_map/psum | solution.py:103
  9.3 233.5 %all-reduce.23.cloned.1.call-start = ((), (), s32[]{:S(2)}) async-start(), calls=%async_computation.10 | async-start | bytes 262144 | tf_op jit(solution)/shard_map/psum | solution.py:82
  26.6 52.7 %copy-start.9 = (s32[1,128]{1,0:T(1,128)S(1)}, s32[1,128]{1,0:T(1,128)}, u32[]{:S(2)}) copy-start(s32[1,128]{1,0:T(1,128)} %param.65) | copy-start | bytes 1540
  26.6 59.3 %copy-start.2 = (f32[128,256]{1,0:T(8,128)S(1)}, f32[128,256]{1,0:T(8,128)}, u32[]{:S(2)}) copy-start(f32[128,256]{1,0:T(8,128)} %param.58) | copy-start | bytes 393220
  26.6 59.3 %copy-start.8 = (f32[128,256]{1,0:T(8,128)S(1)}, f32[128,256]{1,0:T(8,128)}, u32[]{:S(2)}) copy-start(f32[128,256]{1,0:T(8,128)} %param.59) | copy-start | bytes 393220
  26.6 59.3 %copy-start.10 = (f32[256]{0:T(256)S(1)}, f32[256]{0:T(256)}, u32[]{:S(2)}) copy-start(f32[256]{0:T(256)} %param.60) | copy-start | bytes 3076
  76.1 5.4 collective-permute-start
  80.2 5.7 collective-permute-start.1
  169.6 228.7 %copy-start.11 = (f32[128]{0:T(128)}, f32[128]{0:T(128)S(1)}, u32[]{:S(2)}) copy-start(f32[128]{0:T(128)S(1)} %psum.106) | copy-start | bytes 1540
  185.0 135.7 %all-gather.12.cloned.1.call-start = ((), (), s32[]{:S(2)}) async-start(), calls=%async_computation.9 | async-start | bytes 2162688 | tf_op jit(solution)/shard_map/all_gather | solution.py:25
  244.3 154.0 %all-gather.6.cloned.1.call-start = ((), (), s32[]{:S(2)}) async-start(), calls=%async_computation.1 | async-start | bytes 2162688 | tf_op jit(solution)/shard_map/all_gather | solution.py:25
  244.9 293.6 %all-reduce.13.cloned.1.call-start = ((), (), s32[]{:S(2)}) async-start(), calls=%async_computation.2 | async-start | bytes 131072 | tf_op jit(solution)/shard_map/psum | solution.py:103
  398.3 81.4 %copy-start.7 = (bf16[256,128]{1,0:T(8,128)(2,1)S(1)}, bf16[256,128]{1,0:T(8,128)(2,1)}, u32[]{:S(2)}) copy-start(bf16[256,128]{1,0:T(8,128)(2,1)} %param.64) | copy-start | bytes 196612
  480.4 298.2 %all-reduce.15.cloned.1.call-start = ((), (), s32[]{:S(2)}) async-start(), calls=%async_computation.3 | async-start | bytes 131072 | tf_op jit(solution)/shard_map/psum | solution.py:138
  539.3 4.9 collective-permute-start.2
  542.9 5.7 collective-permute-start.3
  720.0 136.3 %all-gather.8.cloned.1.call-start = ((), (), s32[]{:S(2)}) async-start(), calls=%async_computation.4 | async-start | bytes 2162688 | tf_op jit(solution)/shard_map/all_gather | solution.py:25
  778.6 218.5 %all-reduce.17.cloned.1.call-start = ((), (), s32[]{:S(2)}) async-start(), calls=%async_computation.5 | async-start | bytes 131072 | tf_op jit(solution)/shard_map/psum | solution.py:103
  939.1 298.2 %all-reduce.19.cloned.1.call-start = ((), (), s32[]{:S(2)}) async-start(), calls=%async_computation.6 | async-start | bytes 131072 | tf_op jit(solution)/shard_map/psum | solution.py:138
  997.1 10.2 copy-start.4
  998.0 4.9 collective-permute-start.4
  1001.6 5.7 collective-permute-start.5
  1178.8 136.2 %all-gather.10.cloned.1.call-start = ((), (), s32[]{:S(2)}) async-start(), calls=%async_computation.7 | async-start | bytes 2162688 | tf_op jit(solution)/shard_map/all_gather | solution.py:25
  1237.3 218.3 %all-reduce.21.cloned.1.call-start = ((), (), s32[]{:S(2)}) async-start(), calls=%async_computation.8 | async-start | bytes 131072 | tf_op jit(solution)/shard_map/psum | solution.py:103
  1455.7 10.3 copy-start.6
  1456.6 175.3 %copy-start.5 = (f32[128,256]{1,0:T(8,128)S(1)}, f32[128,256]{1,0:T(8,128)}, u32[]{:S(2)}) copy-start(f32[128,256]{1,0:T(8,128)} %get-tuple-element.725) | copy-start | bytes 393220
  1456.6 5.0 collective-permute-start.6
  1460.3 5.7 collective-permute-start.7
Sparse Core Ops, SparseCore 0:
  9.7 65.5 all-reduce.10
  185.1 57.6 all-reduce.22
  245.4 75.2 all-gather.11
  323.1 75.1 all-gather.5
  480.5 57.8 all-reduce.12
  720.2 58.4 all-reduce.14
  781.2 75.1 all-gather.7
  939.3 57.8 all-reduce.16
  1178.9 58.4 all-reduce.18
  1239.8 75.1 all-gather.9
  1397.8 57.8 all-reduce.20
where the time goes:
time: 1650 us; the launch traced here: 1640 us
  waiting for transfers between devices  702 us (43%)
  blocking collectives  674 us (41%)
  matrix products  116 us (7%)
  local copies, waits for them, and re-layouts  91.5 us (6%)
  other arithmetic  20.7 us (1%)
  starting transfers between devices  18.2 us (1%)
    all_gather x4, waiting for transfers between devices, entering(): pieces = jax.tree.map(lambda part: lax.all_gather(part, axis), value)  302 us
    psum x4, blocking collectives, lengths(): lax.psum(jnp.sum(vector * vector, axis=1), ('sec', 'blk')) + epsilon  300 us
    psum x3, blocking collectives, local(): lax.psum(jnp.sum(product[None] * stacked, axis=2), ('sec', 'blk'))  250 us
    psum x4, waiting for transfers between devices, operator(): lax.psum(jnp.dot(rounded, ahead_panel, preferred_element_type=jnp.float32...  207 us
    psum x2, waiting for transfers between devices, local(): lax.psum(jnp.dot(precondition_folded, selector, precision=highest), 'blk')  117 us
    dot_general x93, matrix products, compose(): jnp.dot(first_value, second_map.T, precision=highest) + second_value  97.7 us
    dynamic_slice x186, local copies, waits for them, and re-layouts, step(): longer = join(so_far, jax.tree.map(lambda part: part[position], pieces))  87 us
    all_gather x4, blocking collectives, operator(): lax.all_gather(rounded, 'blk', axis=1, tiled=True)  69.6 us
  transfers between devices with their start and end apart: 19, of which 15 were waited for; matrix products, arithmetic and copies ran while one was open for 1% of the time, Pallas kernels for 0%

commit v1 on v0

--- a/solution.py
+++ b/solution.py
@@ -1,3 +1,4 @@
+import functools
 import jax
 import jax.numpy as jnp
 from jax import lax
@@ -5,6 +6,14 @@
 
 KRYLOV = 3
 epsilon = 1e-06
+
+
+def bind_the_zones(my_data, bus_axis, row_axis):
+    finding = lax.psum(lax.psum(my_data, bus_axis), row_axis)
+    return finding
+
+
+routes_all_edit = functools.partial(bind_the_zones, bus_axis="sec", row_axis="blk")
 
 
 def extended(x, sides, width):
@@ -118,7 +127,7 @@
         return (joined_map, joined_value)
 
     def lengths(vector):
-        return jnp.sqrt(lax.psum(jnp.sum(vector * vector, axis=1), ("sec", "blk")) + epsilon)
+        return jnp.sqrt(routes_all_edit(jnp.sum(vector * vector, axis=1)) + epsilon)
 
     bent = jnp.tanh(state_now)
     residual = source - operator(state_now) - fan_gain[None, :] * bent

time: 1650 us -> 1690 us (1.024)
  blocking collectives: 674 us -> 710 us
    psum x4 -> x8, blocking collectives: 300 us -> 337 us  [bind_the_zones(): finding = lax.psum(lax.psum(my_data, bus_axis), row_axis)]
where the time goes in v1:
time: 1690 us; the launch traced here: 1680 us
  blocking collectives  710 us (42%)
  waiting for transfers between devices  705 us (42%)
  matrix products  116 us (7%)
  local copies, waits for them, and re-layouts  91.5 us (5%)
  other arithmetic  20.7 us (1%)
  starting transfers between devices  18 us (1%)
    psum x8, blocking collectives, bind_the_zones(): finding = lax.psum(lax.psum(my_data, bus_axis), row_axis)  337 us
    all_gather x4, waiting for transfers between devices, entering(): pieces = jax.tree.map(lambda part: lax.all_gather(part, axis), value)  302 us
    psum x3, blocking collectives, local(): lax.psum(jnp.sum(product[None] * stacked, axis=2), ('sec', 'blk'))  250 us
    psum x4, waiting for transfers between devices, operator(): lax.psum(jnp.dot(rounded, ahead_panel, preferred_element_type=jnp.float32...  207 us
    psum x2, waiting for transfers between devices, local(): lax.psum(jnp.dot(precondition_folded, selector, precision=highest), 'blk')  116 us
    dot_general x93, matrix products, compose(): jnp.dot(first_value, second_map.T, precision=highest) + second_value  97.7 us
    dynamic_slice x186, local copies, waits for them, and re-layouts, step(): longer = join(so_far, jax.tree.map(lambda part: part[position], pieces))  87 us
    all_gather x4, blocking collectives, operator(): lax.all_gather(rounded, 'blk', axis=1, tiled=True)  69.6 us
  transfers between devices with their start and end apart: 19, of which 15 were waited for; matrix products, arithmetic and copies ran while one was open for 1% of the time, Pallas kernels for 0%

profile of v1, /device:TPU:1, one launch (start us, length us, event | category | flops | bytes accessed | tf_op | source)
XLA Modules:
  0.0 1679.9 jit_solution(2186722558144076932)
XLA Ops:
  9.4 16.2 all_gather.52
  40.7 34.6 %all-reduce.11.cloned.1.call-done = f32[1,128,128]{1,2,0:T(8,128)} async-done(((f32[1,128,128]{1,2,0:T(8,128)}), f32[1,128,128]{1,2,0:T(8,128)}) %all-reduce.11.cloned.1.call-update) | async-done | bytes 65552 | tf_op jit(solution)/shard_map/psum | solution.py:112
  86.3 59.3 %psum.134 = f32[128]{0:T(128)S(1)} all-reduce(f32[128]{0:T(128)S(1)} %get-tuple-element.720), channel_id=1, replica_groups=mesh['sec'=32,'blk'=8] {'sec'}, use_global_device_ids=true, to_apply=%region_4.0 | all-reduce | flops 128 | bytes 1024 | tf_op jit(solution)/shard_map/psum | solution.py:12
  145.6 29.8 %psum.135 = f32[128]{0:T(128)S(1)} all-reduce(f32[128]{0:T(128)S(1)} %psum.134), channel_id=1, replica_groups=mesh['sec'=32,'blk'=8] {'blk'}, use_global_device_ids=true, to_apply=%region_5.0 | all-reduce | flops 128 | bytes 1024 | tf_op jit(solution)/shard_map/psum | solution.py:12
  175.6 13.6 all_gather.53
  190.7 62.9 %all-reduce.23.cloned.1.call-done = (f32[128,128]{1,0:T(8,128)}, f32[1,128,128]{2,1,0:T(8,128)}) async-done(((f32[128,128]{1,0:T(8,128)}, f32[1,128,128]{2,1,0:T(8,128)}), (f32[128,128]{1,0:T(8,128)}, f32[1,128,128]{2,1,0:T(8,128)})) %all-reduce.23.cloned.1.call-update) | async-done | bytes 131088 | tf_op jit(solution)/shard_map/psum | solution.py:91
  255.7 75.7 %all-gather.12.cloned.1.call-done = f32[4096,128]{1,0:T(8,128)} async-done(((f32[128,128]{1,0:T(8,128)}), f32[4096,128]{1,0:T(8,128)}) %all-gather.12.cloned.1.call-update) | async-done | bytes 2097168 | tf_op jit(solution)/shard_map/all_gather | solution.py:34
  331.4 77.6 %all-gather.6.cloned.1.call-done = f32[32,128,128]{2,1,0:T(8,128)} async-done(((f32[1,128,128]{2,1,0:T(8,128)}), f32[32,128,128]{2,1,0:T(8,128)}) %all-gather.6.cloned.1.call-update) | async-done | bytes 2097168 | tf_op jit(solution)/shard_map/all_gather | solution.py:34
  409.0 63.2 %while.64 = (s32[]{:T(128)}, f32[128,128]{0,1:T(8,128)S(1)}, s32[]{:T(128)}, f32[32,128,128]{2,1,0:T(8,128)}, f32[32,128,128]{2,1,0:T(8,128)}, /*index=5*/s32[]{:T(128)}, s32[]{:T(128)}) while((s32[]{:T(128)}, f32[128,128]{0,1:T(8,128)S(1)}, s32[]{:T(128)}, f32[32,128,128]{2,1,0:T(8,128)}, f32[32,128,128]{2,1,0:T(8,128)}, ...), condition=%wide.region_9.10_spmd.clone, body=%wide.region_8.9_spmd.clone.sunk | while | flops 25231364 | bytes 723043 | solution.py:43
  472.6 17.8 %all_gather.59 = bf16[128,2048]{1,0:T(8,128)(2,1)S(1)} all-gather(bf16[128,256]{1,0:T(8,128)(2,1)S(1)} %get-tuple-element.722), channel_id=1, replica_groups=mesh['sec'=32,'blk'=8] {'blk'}, dimensions={1}, use_global_device_ids=true | all-gather | bytes 589824 | tf_op jit(solution)/shard_map/all_gather | solution.py:110
  491.6 57.6 %all-reduce.13.cloned.1.call-done = f32[1,128,128]{2,1,0:T(8,128)} async-done(((f32[1,128,128]{2,1,0:T(8,128)}), f32[1,128,128]{2,1,0:T(8,128)}) %all-reduce.13.cloned.1.call-update) | async-done | bytes 65552 | tf_op jit(solution)/shard_map/psum | solution.py:112
  559.8 83.2 %psum.139 = f32[1,128]{1,0:T(1,128)S(1)} all-reduce(f32[1,128]{1,0:T(1,128)S(1)} %bitcast.287), channel_id=1, replica_groups=mesh['sec'=32,'blk'=8] {'sec','blk'}, use_global_device_ids=true, to_apply=%region_12.13 | all-reduce | flops 128 | bytes 1024 | tf_op jit(solution)/shard_map/psum | solution.py:158
  643.3 55.8 %psum.140 = f32[128]{0:T(128)S(1)} all-reduce(f32[128]{0:T(128)S(1)} %get-tuple-element.687), channel_id=1, replica_groups=mesh['sec'=32,'blk'=8] {'sec'}, use_global_device_ids=true, to_apply=%region_14.15 | all-reduce | flops 128 | bytes 1024 | tf_op jit(solution)/shard_map/psum | solution.py:12
  699.1 26.6 %psum.141 = f32[128]{0:T(128)S(1)} all-reduce(f32[128]{0:T(128)S(1)} %psum.140), channel_id=1, replica_groups=mesh['sec'=32,'blk'=8] {'blk'}, use_global_device_ids=true, to_apply=%region_15.16 | all-reduce | flops 128 | bytes 1024 | tf_op jit(solution)/shard_map/psum | solution.py:12
  725.8 13.6 all_gather.60
  740.9 57.7 %all-reduce.15.cloned.1.call-done = f32[1,128,128]{2,1,0:T(8,128)} async-done(((f32[1,128,128]{2,1,0:T(8,128)}), f32[1,128,128]{2,1,0:T(8,128)}) %all-reduce.15.cloned.1.call-update) | async-done | bytes 65552 | tf_op jit(solution)/shard_map/psum | solution.py:147
  798.8 77.7 %all-gather.8.cloned.1.call-done = f32[32,128,128]{2,1,0:T(8,128)} async-done(((f32[1,128,128]{2,1,0:T(8,128)}), f32[32,128,128]{2,1,0:T(8,128)}) %all-gather.8.cloned.1.call-update) | async-done | bytes 2097168 | tf_op jit(solution)/shard_map/all_gather | solution.py:34
  876.4 63.2 %while.65 = (s32[]{:T(128)}, f32[128,128]{0,1:T(8,128)S(1)}, s32[]{:T(128)}, f32[32,128,128]{2,1,0:T(8,128)}, f32[32,128,128]{2,1,0:T(8,128)}, /*index=5*/s32[]{:T(128)}, s32[]{:T(128)}) while((s32[]{:T(128)}, f32[128,128]{0,1:T(8,128)S(1)}, s32[]{:T(128)}, f32[32,128,128]{2,1,0:T(8,128)}, f32[32,128,128]{2,1,0:T(8,128)}, ...), condition=%wide.region_18.19_spmd.clone, body=%wide.region_17.18_spmd.clone.sunk | while | flops 25231364 | bytes 723043 | solution.py:43
  940.6 17.8 %all_gather.63 = bf16[128,2048]{1,0:T(8,128)(2,1)S(1)} all-gather(bf16[128,256]{1,0:T(8,128)(2,1)S(1)} %get-tuple-element.724), channel_id=1, replica_groups=mesh['sec'=32,'blk'=8] {'blk'}, dimensions={1}, use_global_device_ids=true | all-gather | bytes 589824 | tf_op jit(solution)/shard_map/all_gather | solution.py:110
  959.6 57.6 %all-reduce.17.cloned.1.call-done = f32[1,128,128]{2,1,0:T(8,128)} async-done(((f32[1,128,128]{2,1,0:T(8,128)}), f32[1,128,128]{2,1,0:T(8,128)}) %all-reduce.17.cloned.1.call-update) | async-done | bytes 65552 | tf_op jit(solution)/shard_map/psum | solution.py:112
  1027.8 83.4 %psum.144 = f32[2,128]{1,0:T(2,128)S(1)} all-reduce(f32[2,128]{1,0:T(2,128)S(1)} %multiply_reduce_fusion.3), channel_id=1, replica_groups=mesh['sec'=32,'blk'=8] {'sec','blk'}, use_global_device_ids=true, to_apply=%region_21.22 | all-reduce | flops 256 | bytes 2048 | tf_op jit(solution)/shard_map/psum | solution.py:158
  1111.5 55.8 %psum.145 = f32[128]{0:T(128)S(1)} all-reduce(f32[128]{0:T(128)S(1)} %get-tuple-element.683), channel_id=1, replica_groups=mesh['sec'=32,'blk'=8] {'sec'}, use_global_device_ids=true, to_apply=%region_24.25 | all-reduce | flops 128 | bytes 1024 | tf_op jit(solution)/shard_map/psum | solution.py:12
  1167.3 26.6 %psum.146 = f32[128]{0:T(128)S(1)} all-reduce(f32[128]{0:T(128)S(1)} %psum.145), channel_id=1, replica_groups=mesh['sec'=32,'blk'=8] {'blk'}, use_global_device_ids=true, to_apply=%region_25.26 | all-reduce | flops 128 | bytes 1024 | tf_op jit(solution)/shard_map/psum | solution.py:12
  1194.1 13.6 all_gather.64
  1209.2 57.8 %all-reduce.19.cloned.1.call-done = f32[1,128,128]{2,1,0:T(8,128)} async-done(((f32[1,128,128]{2,1,0:T(8,128)}), f32[1,128,128]{2,1,0:T(8,128)}) %all-reduce.19.cloned.1.call-update) | async-done | bytes 65552 | tf_op jit(solution)/shard_map/psum | solution.py:147
  1273.5 71.1 %all-gather.10.cloned.1.call-done = f32[32,128,128]{2,1,0:T(8,128)} async-done(((f32[1,128,128]{2,1,0:T(8,128)}), f32[32,128,128]{2,1,0:T(8,128)}) %all-gather.10.cloned.1.call-update) | async-done | bytes 2097168 | tf_op jit(solution)/shard_map/all_gather | solution.py:34
  1344.6 63.2 %while.66 = (s32[]{:T(128)}, f32[128,128]{0,1:T(8,128)S(1)}, s32[]{:T(128)}, f32[32,128,128]{2,1,0:T(8,128)}, f32[32,128,128]{2,1,0:T(8,128)}, /*index=5*/s32[]{:T(128)}, s32[]{:T(128)}) while((s32[]{:T(128)}, f32[128,128]{0,1:T(8,128)S(1)}, s32[]{:T(128)}, f32[32,128,128]{2,1,0:T(8,128)}, f32[32,128,128]{2,1,0:T(8,128)}, ...), condition=%wide.region_29.30_spmd.clone, body=%wide.region_28.29_spmd.clone.sunk | while | flops 25231364 | bytes 723043 | solution.py:43
  1408.7 17.8 %all_gather.67 = bf16[128,2048]{1,0:T(8,128)(2,1)S(1)} all-gather(bf16[128,256]{1,0:T(8,128)(2,1)S(1)} %get-tuple-element.726), channel_id=1, replica_groups=mesh['sec'=32,'blk'=8] {'blk'}, dimensions={1}, use_global_device_ids=true | all-gather | bytes 589824 | tf_op jit(solution)/shard_map/all_gather | solution.py:110
  1427.7 57.6 %all-reduce.21.cloned.1.call-done = f32[1,128,128]{2,1,0:T(8,128)} async-done(((f32[1,128,128]{2,1,0:T(8,128)}), f32[1,128,128]{2,1,0:T(8,128)}) %all-reduce.21.cloned.1.call-update) | async-done | bytes 65552 | tf_op jit(solution)/shard_map/psum | solution.py:112
  1496.8 83.2 %psum.149 = f32[3,128]{1,0:T(4,128)S(1)} all-reduce(f32[3,128]{1,0:T(4,128)S(1)} %multiply_reduce_fusion.1), channel_id=1, replica_groups=mesh['sec'=32,'blk'=8] {'sec','blk'}, use_global_device_ids=true, to_apply=%region_32.33 | all-reduce | flops 384 | bytes 3072 | tf_op jit(solution)/shard_map/psum | solution.py:158
  1580.2 55.8 %psum.150 = f32[128]{0:T(128)S(1)} all-reduce(f32[128]{0:T(128)S(1)} %multiply_reduce_fusion.4), channel_id=1, replica_groups=mesh['sec'=32,'blk'=8] {'sec'}, use_global_device_ids=true, to_apply=%region_35.36 | all-reduce | flops 128 | bytes 1024 | tf_op jit(solution)/shard_map/psum | solution.py:12
  1636.1 26.6 %psum.151 = f32[128]{0:T(128)S(1)} all-reduce(f32[128]{0:T(128)S(1)} %psum.150), channel_id=1, replica_groups=mesh['sec'=32,'blk'=8] {'blk'}, use_global_device_ids=true, to_apply=%region_36.37 | all-reduce | flops 128 | bytes 1024 | tf_op jit(solution)/shard_map/psum | solution.py:12
  (525 shorter events, 277.3 us)
Async XLA Ops:
  6.5 33.7 %copy-start = (bf16[256,2048]{1,0:T(8,128)(2,1)S(1)}, bf16[256,2048]{1,0:T(8,128)(2,1)}, u32[]{:S(2)}) copy-start(bf16[256,2048]{1,0:T(8,128)(2,1)} %param.62) | copy-start | bytes 3145732
  6.5 20.0 %copy-start.1 = (bf16[256,2048]{1,0:T(8,128)(2,1)S(1)}, bf16[256,2048]{1,0:T(8,128)(2,1)}, u32[]{:S(2)}) copy-start(bf16[256,2048]{1,0:T(8,128)(2,1)} %param.61) | copy-start | bytes 3145732
  6.5 20.6 %copy-start.3 = (bf16[256,128]{1,0:T(8,128)(2,1)S(1)}, bf16[256,128]{1,0:T(8,128)(2,1)}, u32[]{:S(2)}) copy-start(bf16[256,128]{1,0:T(8,128)(2,1)} %param.63) | copy-start | bytes 196612
  6.5 68.7 %all-reduce.11.cloned.1.call-start = ((), (), s32[]{:S(2)}) async-start(), calls=%async_computation | async-start | bytes 131072 | tf_op jit(solution)/shard_map/psum | solution.py:112
  9.3 244.2 %all-reduce.23.cloned.1.call-start = ((), (), s32[]{:S(2)}) async-start(), calls=%async_computation.10 | async-start | bytes 262144 | tf_op jit(solution)/shard_map/psum | solution.py:91
  26.6 52.7 %copy-start.9 = (s32[1,128]{1,0:T(1,128)S(1)}, s32[1,128]{1,0:T(1,128)}, u32[]{:S(2)}) copy-start(s32[1,128]{1,0:T(1,128)} %param.65) | copy-start | bytes 1540
  26.6 59.3 %copy-start.2 = (f32[128,256]{1,0:T(8,128)S(1)}, f32[128,256]{1,0:T(8,128)}, u32[]{:S(2)}) copy-start(f32[128,256]{1,0:T(8,128)} %param.58) | copy-start | bytes 393220
  26.6 59.3 %copy-start.8 = (f32[128,256]{1,0:T(8,128)S(1)}, f32[128,256]{1,0:T(8,128)}, u32[]{:S(2)}) copy-start(f32[128,256]{1,0:T(8,128)} %param.59) | copy-start | bytes 393220
  26.6 59.3 %copy-start.10 = (f32[256]{0:T(256)S(1)}, f32[256]{0:T(256)}, u32[]{:S(2)}) copy-start(f32[256]{0:T(256)} %param.60) | copy-start | bytes 3076
  76.1 5.4 collective-permute-start
  80.2 5.7 collective-permute-start.1
  175.5 233.5 %copy-start.11 = (f32[128]{0:T(128)}, f32[128]{0:T(128)S(1)}, u32[]{:S(2)}) copy-start(f32[128]{0:T(128)S(1)} %psum.135) | copy-start | bytes 1540
  190.6 140.8 %all-gather.12.cloned.1.call-start = ((), (), s32[]{:S(2)}) async-start(), calls=%async_computation.9 | async-start | bytes 2162688 | tf_op jit(solution)/shard_map/all_gather | solution.py:34
  255.0 154.0 %all-gather.6.cloned.1.call-start = ((), (), s32[]{:S(2)}) async-start(), calls=%async_computation.1 | async-start | bytes 2162688 | tf_op jit(solution)/shard_map/all_gather | solution.py:34
  255.6 293.6 %all-reduce.13.cloned.1.call-start = ((), (), s32[]{:S(2)}) async-start(), calls=%async_computation.2 | async-start | bytes 131072 | tf_op jit(solution)/shard_map/psum | solution.py:112
  409.0 81.4 %copy-start.7 = (bf16[256,128]{1,0:T(8,128)(2,1)S(1)}, bf16[256,128]{1,0:T(8,128)(2,1)}, u32[]{:S(2)}) copy-start(bf16[256,128]{1,0:T(8,128)(2,1)} %param.64) | copy-start | bytes 196612
  491.2 307.5 %all-reduce.15.cloned.1.call-start = ((), (), s32[]{:S(2)}) async-start(), calls=%async_computation.3 | async-start | bytes 131072 | tf_op jit(solution)/shard_map/psum | solution.py:147
  550.0 4.9 collective-permute-start.2
  553.6 5.7 collective-permute-start.3
  740.9 135.5 %all-gather.8.cloned.1.call-start = ((), (), s32[]{:S(2)}) async-start(), calls=%async_computation.4 | async-start | bytes 2162688 | tf_op jit(solution)/shard_map/all_gather | solution.py:34
  798.7 218.5 %all-reduce.17.cloned.1.call-start = ((), (), s32[]{:S(2)}) async-start(), calls=%async_computation.5 | async-start | bytes 131072 | tf_op jit(solution)/shard_map/psum | solution.py:112
  959.2 307.7 %all-reduce.19.cloned.1.call-start = ((), (), s32[]{:S(2)}) async-start(), calls=%async_computation.6 | async-start | bytes 131072 | tf_op jit(solution)/shard_map/psum | solution.py:147
  1017.2 10.2 copy-start.4
  1018.1 4.9 collective-permute-start.4
  1021.7 5.7 collective-permute-start.5
  1209.1 135.4 %all-gather.10.cloned.1.call-start = ((), (), s32[]{:S(2)}) async-start(), calls=%async_computation.7 | async-start | bytes 2162688 | tf_op jit(solution)/shard_map/all_gather | solution.py:34
  1267.0 218.3 %all-reduce.21.cloned.1.call-start = ((), (), s32[]{:S(2)}) async-start(), calls=%async_computation.8 | async-start | bytes 131072 | tf_op jit(solution)/shard_map/psum | solution.py:112
  1485.3 10.3 copy-start.6
  1486.2 185.5 %copy-start.5 = (f32[128,256]{1,0:T(8,128)S(1)}, f32[128,256]{1,0:T(8,128)}, u32[]{:S(2)}) copy-start(f32[128,256]{1,0:T(8,128)} %get-tuple-element.725) | copy-start | bytes 393220
  1486.2 5.0 collective-permute-start.6
  1489.9 5.7 collective-permute-start.7
Sparse Core Ops, SparseCore 0:
  9.7 65.5 all-reduce.10
  190.7 62.7 all-reduce.22
  256.1 75.2 all-gather.11
  333.8 75.1 all-gather.5
  491.3 57.8 all-reduce.12
  741.0 57.6 all-reduce.14
  801.3 75.1 all-gather.7
  959.3 57.8 all-reduce.16
  1209.2 57.6 all-reduce.18
  1269.4 75.1 all-gather.9
  1427.4 57.8 all-reduce.20
